TPU v7x, 32 devices: a whole 2x2x4 slice. The times are simulated.
32 devices in a mesh: crop: 8 (over z, x), shard: 4 (over y, core).
Axes of the slice: x: 2, y: 2, z: 4, core: 2. Of those that a mesh axis runs over, the one named last changes fastest.
Arguments:
- master: float32 [14320, 128], P('shard')
- first_moment: float32 [14320, 128], P('shard'), may hold values from -5.722046e-06 to 5.722046e-06
- second_moment: float32 [14320, 128], P('shard'), may hold values from 6.8195707e-15 to 1.0911313e-13
- step: int32 [1], replicated, may hold values from 2 to 20
- plm_table: bfloat16 [21, 1280], replicated, may hold values from -6 to 6
- plm_first: bfloat16 [1280, 5248], P('shard'), may hold values from -0.15625 to 0.15625
- plm_second: bfloat16 [2560, 1280], P('shard'), may hold values from -0.25 to 0.25
- tokens: int32 [512, 32], P(('crop', 'shard')), may hold values from 0 to 20
- lengths: int32 [512], P(('crop', 'shard')), may hold values from 12 to 32
- resolved: int32 [512, 32], P(('crop', 'shard')), may hold values 0 or 1
- coords: float32 [512, 3, 32], P(('crop', 'shard')), may hold values from -15 to 15
Outputs:
- new_master: float32 [14320, 128], P('shard')
- new_first: float32 [14320, 128], P('shard')
- new_second: float32 [14320, 128], P('shard')
- weights_low: bfloat16 [14320, 128], P('shard')
- loss: float32 [], replicated
- grad_norm: float32 [], replicated
All inputs are finite; a program needn't handle non-finite values. No bound on the sum of `resolved` on one device may be relied on, other than what follows from the above.
Results may differ from a plain program's by a relative error of at most 0.012.
The roundings to bfloat16 on the way count: a program that leaves them out, or rounds other values in their place, can miss the bound.
Values may be sent and summed in bfloat16 or wider, within the bound.
No kernel may reach another device: no remote copies, remote signals or barrier semaphores. Data moves between devices by JAX's collectives and lax.ppermute only.
A program may use at most 320 MiB of HBM per device.

v0:
```python
import jax
import jax.numpy as jnp
from jax import lax
from jax.sharding import PartitionSpec as P

NODE = 256
PAIR = 128
HEADS = 8
PAIR_HEADS = 4
PLM = 1280
PLM_FF = 2560
PLM_Z = 128
NODE_FF = 1024
PAIR_FF = 512
VOCAB = 21
BINS = 65
IPA_PTS = 4
RES = 32
MICRO = 4
beta_one = 0.9
beta_two = 0.999
learn_rate = 0.02
adam_eps = 1e-10
decay_rate = 0.01
clip_norm = 0.005
point_weight = 0.01


def layout():
    return [
        ("w_in", (PLM, NODE)),
        ("w_qkv", (NODE, 3 * NODE)),
        ("w_out", (NODE, NODE)),
        ("w_lr", (NODE, 2 * PAIR)),
        ("w_n1", (NODE, NODE_FF)),
        ("w_n2", (NODE_FF, NODE)),
        ("w_bias", (PAIR, HEADS)),
        ("w_op", (PAIR, PAIR)),
        ("w_tri", (PAIR, 5 * PAIR)),
        ("w_tri_out", (PAIR, PAIR)),
        ("w_pa", (PAIR, 4 * PAIR)),
        ("w_pa_out", (PAIR, PAIR)),
        ("w_p1", (PAIR, PAIR_FF)),
        ("w_p2", (PAIR_FF, PAIR)),
        ("w_rel", (BINS, PAIR)),
        ("w_s", (NODE, 3)),
        ("w_ipa", (NODE, 3 * NODE)),
        ("w_pts", (NODE, 6 * HEADS * IPA_PTS)),
        ("w_ipa_bias", (PAIR, HEADS)),
        ("w_ipa_out", (NODE, NODE)),
        ("w_bb", (NODE, 3)),
        ("g_node", (6, NODE)),
        ("g_pair", (6, PAIR)),
    ]


def unpack(flat):
    params = {}
    offset = 0
    for weight_name, extent in layout():
        entries = extent[0] * extent[1]
        params[weight_name] = flat[offset : offset + entries].reshape(extent)
        offset += entries
    return params


def pack(params, total):
    flat = jnp.concatenate([params[weight_name].reshape(-1) for weight_name, extent in layout()])
    return jnp.pad(flat, (0, total - flat.shape[0])).reshape(-1, 128)


def product(form, left, right):
    return jnp.einsum(
        form,
        left.astype(jnp.bfloat16),
        right.astype(jnp.bfloat16),
        preferred_element_type=jnp.float32,
    )


def passthrough(values):
    return values


def layer_norm(values, gain):
    centred = values - jnp.mean(values, axis=-1, keepdims=True)
    spread = jnp.mean(centred * centred, axis=-1, keepdims=True)
    return centred * lax.rsqrt(spread + 1e-05) * gain


def softmax_last(scores):
    expo = jnp.exp(scores - jnp.max(scores, axis=-1, keepdims=True))
    return expo / jnp.sum(expo, axis=-1, keepdims=True)


def residue_weight(lengths, resolved):
    positions = jnp.arange(resolved.shape[1])
    valid = (positions[None, :] < lengths[:, None]).astype(jnp.float32)
    first = (positions == 0).astype(jnp.float32)[None, :]
    return (jnp.maximum(resolved.astype(jnp.float32), first) * valid, valid)


def crop_loss(
    params,
    table,
    plm_first,
    plm_second,
    tokens,
    lengths,
    resolved,
    coords,
    inv_count,
    multiply,
    round_fn,
):
    crops, residues = tokens.shape
    positions = jnp.arange(residues)
    weight_res, valid = residue_weight(lengths, resolved)
    key_mask = valid[:, None, :] > 0
    pmask = (valid[:, :, None] * valid[:, None, :])[..., None]
    one_hot = (tokens[:, :, None] == jnp.arange(VOCAB)[None, None, :]).astype(jnp.float32)
    features = multiply("crv,vp->crp", one_hot, table)
    uvz = jax.nn.silu(multiply("crp,pe->cre", round_fn(layer_norm(features, 1.0)), plm_first))
    base = round_fn(uvz[..., 2 * PLM_FF :])
    plm_scores = jnp.where(
        key_mask, multiply("ciz,cjz->cij", base, base) * PLM_Z ** (-0.5), -1000000000.0
    )
    mixed = multiply(
        "cij,cje->cie", round_fn(softmax_last(plm_scores)), round_fn(uvz[..., PLM_FF : 2 * PLM_FF])
    )
    plm_out = features + multiply("cie,ep->cip", round_fn(uvz[..., :PLM_FF] * mixed), plm_second)
    node = multiply("crp,pn->crn", round_fn(layer_norm(plm_out, 1.0)), params["w_in"])
    offsets = jnp.clip(positions[None, :] - positions[:, None] + (BINS - 1) // 2, 0, BINS - 1)
    rel_hot = (offsets[:, :, None] == jnp.arange(BINS)[None, None, :]).astype(jnp.float32)
    pair = jnp.broadcast_to(
        multiply("ijb,bp->ijp", rel_hot, params["w_rel"])[None], (crops, residues, residues, PAIR)
    )
    gain_node, gain_pair = (params["g_node"], params["g_pair"])
    sides = multiply("crn,nq->crq", round_fn(layer_norm(node, gain_node[0])), params["w_lr"])
    outer = sides[:, :, None, :PAIR] * sides[:, None, :, PAIR:]
    pair = pair + multiply("cijp,pq->cijq", round_fn(outer), params["w_op"])
    tri_proj = multiply("cijp,pq->cijq", round_fn(layer_norm(pair, gain_pair[0])), params["w_tri"])
    tri_left = jax.nn.sigmoid(tri_proj[..., :PAIR]) * tri_proj[..., PAIR : 2 * PAIR] * pmask
    tri_right = (
        jax.nn.sigmoid(tri_proj[..., 2 * PAIR : 3 * PAIR])
        * tri_proj[..., 3 * PAIR : 4 * PAIR]
        * pmask
    )
    tri = multiply("cikp,cjkp->cijp", round_fn(tri_left), round_fn(tri_right))
    tri_update = multiply(
        "cijp,pq->cijq", round_fn(layer_norm(tri, gain_pair[1])), params["w_tri_out"]
    )
    pair = pair + jax.nn.sigmoid(tri_proj[..., 4 * PAIR :]) * tri_update
    pair_dim = PAIR // PAIR_HEADS
    pa_proj = multiply("cijp,pq->cijq", round_fn(layer_norm(pair, gain_pair[2])), params["w_pa"])
    pa_qkv = round_fn(pa_proj[..., : 3 * PAIR])
    pa_query = pa_qkv[..., :PAIR].reshape(crops, residues, residues, PAIR_HEADS, pair_dim)
    pa_keys = pa_qkv[..., PAIR : 2 * PAIR].reshape(crops, residues, residues, PAIR_HEADS, pair_dim)
    pa_values = pa_qkv[..., 2 * PAIR :].reshape(crops, residues, residues, PAIR_HEADS, pair_dim)
    pa_scores = multiply("cijhd,cikhd->cihjk", pa_query, pa_keys) * pair_dim ** (-0.5)
    pa_scores = jnp.where(valid[:, None, None, None, :] > 0, pa_scores, -1000000000.0)
    pa_out = multiply("cihjk,cikhd->cijhd", round_fn(softmax_last(pa_scores)), pa_values).reshape(
        crops, residues, residues, PAIR
    )
    pair = pair + multiply(
        "cijp,pq->cijq",
        round_fn(jax.nn.sigmoid(pa_proj[..., 3 * PAIR :]) * pa_out),
        params["w_pa_out"],
    )
    hidden = jax.nn.gelu(
        multiply("cijp,pf->cijf", round_fn(layer_norm(pair, gain_pair[3])), params["w_p1"]),
        approximate=True,
    )
    pair = pair + multiply("cijf,fp->cijp", round_fn(hidden), params["w_p2"])
    bias = multiply("cijp,ph->chij", round_fn(layer_norm(pair, gain_pair[4])), params["w_bias"])
    head_dim = NODE // HEADS
    qkv = round_fn(
        multiply("crn,nq->crq", round_fn(layer_norm(node, gain_node[1])), params["w_qkv"])
    )
    query = qkv[..., :NODE].reshape(crops, residues, HEADS, head_dim)
    keys = qkv[..., NODE : 2 * NODE].reshape(crops, residues, HEADS, head_dim)
    values = qkv[..., 2 * NODE :].reshape(crops, residues, HEADS, head_dim)
    scores = multiply("cihd,cjhd->chij", query, keys) * head_dim ** (-0.5) + bias
    scores = jnp.where(valid[:, None, None, :] > 0, scores, -1000000000.0)
    attended = multiply("chij,cjhd->cihd", round_fn(softmax_last(scores)), values).reshape(
        crops, residues, NODE
    )
    node = node + multiply("crn,nm->crm", round_fn(attended), params["w_out"])
    hidden_node = jax.nn.gelu(
        multiply("crn,nf->crf", round_fn(layer_norm(node, gain_node[2])), params["w_n1"]),
        approximate=True,
    )
    node = node + multiply("crf,fn->crn", round_fn(hidden_node), params["w_n2"])
    start_pos = multiply("crn,nk->crk", round_fn(layer_norm(node, gain_node[3])), params["w_s"])
    single = round_fn(layer_norm(node, gain_node[4]))
    sqkv = round_fn(multiply("crn,nq->crq", single, params["w_ipa"]))
    s_query = sqkv[..., :NODE].reshape(crops, residues, HEADS, head_dim)
    s_keys = sqkv[..., NODE : 2 * NODE].reshape(crops, residues, HEADS, head_dim)
    s_values = sqkv[..., 2 * NODE :].reshape(crops, residues, HEADS, head_dim)
    points = round_fn(multiply("crn,nq->crq", single, params["w_pts"])).reshape(
        crops, residues, 2, HEADS, IPA_PTS, 3
    )
    points = points + start_pos[:, :, None, None, None, :]
    point_diff = points[:, :, None, 0] - points[:, None, :, 1]
    dist = jnp.transpose(jnp.sum(point_diff * point_diff, axis=(-1, -2)), (0, 3, 1, 2))
    ipa_bias = multiply(
        "cijp,ph->chij", round_fn(layer_norm(pair, gain_pair[5])), params["w_ipa_bias"]
    )
    ipa_scores = (
        multiply("cihd,cjhd->chij", s_query, s_keys) * head_dim ** (-0.5)
        + ipa_bias
        - point_weight * dist
    )
    ipa_scores = jnp.where(valid[:, None, None, :] > 0, ipa_scores, -1000000000.0)
    ipa_att = multiply("chij,cjhd->cihd", round_fn(softmax_last(ipa_scores)), s_values).reshape(
        crops, residues, NODE
    )
    node = node + multiply("crn,nm->crm", round_fn(ipa_att), params["w_ipa_out"])
    predicted = start_pos + multiply(
        "crn,nk->crk", round_fn(layer_norm(node, gain_node[5])), params["w_bb"]
    )
    truth = jnp.transpose(coords, (0, 2, 1))
    pred_diff = predicted[:, :, None, :] - predicted[:, None, :, :]
    true_diff = truth[:, :, None, :] - truth[:, None, :, :]
    dist_pred = jnp.sqrt(jnp.sum(pred_diff * pred_diff, axis=-1) + 1.0)
    dist_true = jnp.sqrt(jnp.sum(true_diff * true_diff, axis=-1) + 1.0)
    error = jnp.sqrt((dist_pred - dist_true) ** 2 + 1.0) - 1.0
    pair_weight = weight_res[:, :, None] * weight_res[:, None, :]
    return jnp.sum(pair_weight * error) * inv_count


def adam_update(master, first_moment, second_moment, step, grad, norm):
    clipped = grad * jnp.minimum(1.0, clip_norm / norm)
    first = beta_one * first_moment + (1.0 - beta_one) * clipped
    second = beta_two * second_moment + (1.0 - beta_two) * clipped * clipped
    step_count = step[0].astype(jnp.float32)
    first_hat = first / (1.0 - beta_one**step_count)
    second_hat = second / (1.0 - beta_two**step_count)
    updated = master - learn_rate * (
        first_hat / (jnp.sqrt(second_hat) + adam_eps) + decay_rate * master
    )
    return (updated, first, second, updated.astype(jnp.bfloat16))


def local(
    master,
    first_moment,
    second_moment,
    step,
    plm_table,
    plm_first,
    plm_second,
    tokens,
    lengths,
    resolved,
    coords,
):
    gathered, frozen_first, frozen_second = (
        lax.all_gather(master.astype(jnp.bfloat16), "shard", axis=0, tiled=True),
        lax.all_gather(plm_first, "shard", axis=0, tiled=True),
        lax.all_gather(plm_second, "shard", axis=0, tiled=True),
    )
    params = unpack(gathered.astype(jnp.float32).reshape(-1))
    weight_res, valid = residue_weight(lengths, resolved)
    local_pairs = jnp.sum(jnp.sum(weight_res, axis=1) ** 2)
    total_pairs = lax.psum(local_pairs, ("crop", "shard"))
    inv_count = 1.0 / total_pairs
    per_micro = tokens.shape[0] // MICRO
    batches = (
        tokens.reshape(MICRO, per_micro, RES),
        lengths.reshape(MICRO, per_micro),
        resolved.reshape(MICRO, per_micro, RES),
        coords.reshape(MICRO, per_micro, 3, RES),
    )

    def micro_step(carry, batch):
        micro_tokens, micro_lengths, micro_resolved, micro_coords = batch

        def loss_of(weights):
            return crop_loss(
                weights,
                plm_table,
                frozen_first,
                frozen_second,
                micro_tokens,
                micro_lengths,
                micro_resolved,
                micro_coords,
                inv_count,
                product,
                passthrough,
            )

        value, pullback = jax.vjp(loss_of, params)
        (grads,) = pullback(jnp.float32(1.0))
        return ((jax.tree.map(jnp.add, carry[0], grads), carry[1] + value), None)

    empty_grads = jax.tree.map(jnp.zeros_like, params)
    (grads, loss_part), unused = lax.scan(micro_step, (empty_grads, jnp.float32(0.0)), batches)
    grad_rows = pack(grads, gathered.size)
    own_rows = master.shape[0]
    summed, loss = lax.psum((grad_rows, loss_part), ("crop", "shard"))
    own_grad = lax.dynamic_slice_in_dim(summed, lax.axis_index("shard") * own_rows, own_rows, 0)
    norm = jnp.sqrt(jnp.sum(summed * summed))
    updated, first, second, copy_low = adam_update(
        master, first_moment, second_moment, step, own_grad, norm
    )
    return (updated, first, second, copy_low, loss, norm)


def solution(mesh):
    placed = (
        P("shard", None),
        P("shard", None),
        P("shard", None),
        P(),
        P(),
        P("shard", None),
        P("shard", None),
        P(("crop", "shard"), None),
        P(("crop", "shard")),
        P(("crop", "shard"), None),
        P(("crop", "shard"), None, None),
    )
    return jax.shard_map(
        local,
        mesh=mesh,
        in_specs=placed,
        out_specs=(
            P("shard", None),
            P("shard", None),
            P("shard", None),
            P("shard", None),
            P(),
            P(),
        ),
        check_vma=False,
    )
```

profile of v0, /device:TPU:0, one launch (start us, length us, event | category | flops | bytes accessed | tf_op | source)
XLA Modules:
  0.0 2196.8 jit_solution(18156242039349124732)
XLA Ops:
  12.1 42.6 %psum.21 = f32[]{:T(128)} all-reduce(f32[]{:T(128)} %multiply_reduce_fusion.27), channel_id=1, replica_groups=mesh['crop'=8,'shard'=4] {'crop','shard'}, use_global_device_ids=true, to_apply=%region_2.0 | all-reduce | flops 1 | bytes 8 | tf_op jit(solution)/shard_map/psum | solution.py:266
  80.9 13.3 all-gather.7.cloned.1.call-done
  94.2 88.5 %all-gather.5.cloned.1.call-done = bf16[1280,5248]{1,0:T(8,128)(2,1)} async-done(((bf16[320,5248]{1,0:T(8,128)(2,1)}), bf16[1280,5248]{1,0:T(8,128)(2,1)}) %all-gather.5.cloned.1.call-update) | async-done | bytes 13434896 | tf_op jit(solution)/shard_map/all_gather | solution.py:260
  182.7 1802.7 %while.60 = (s32[]{:T(128)}, f32[6,256]{1,0:T(8,128)}, f32[6,128]{1,0:T(8,128)}, f32[256,3]{0,1:T(4,128)}, f32[128,8]{0,1:T(8,128)}, /*index=5*/f32[1280,256]{1,...) while((s32[]{:T(128)}, f32[6,256]{1,0:T(8,128)}, ...), condition=%wide.region_91.92_spmd.clone, body=%wide.region_3.91_spmd.clone.sunk | while | flops 12452269056 | bytes 911625600 | solution.py:299
  189.1 9.2 fusion.776
  218.9 7.2 copy.876
  226.2 7.2 copy.877
  233.4 9.0 bitcast_reduce_fusion.2
  242.4 8.0 copy.878
  472.6 12.2 convert_reduce_fusion.6
  484.8 9.2 convolution_convert_fusion.47
  498.7 10.0 fusion.843
  508.8 8.5 convert_bitcast_fusion.6
  517.3 10.0 convert_bitcast_fusion.5
  527.2 8.5 copy.901
  541.9 8.4 copy.902
  579.4 6.3 copy.904
  585.7 6.8 fusion.852
  635.5 9.2 fusion.776
  665.1 7.2 copy.876
  672.3 7.2 copy.877
  679.5 9.0 bitcast_reduce_fusion.2
  688.5 8.0 copy.878
  921.6 12.4 convert_reduce_fusion.6
  934.0 9.2 convolution_convert_fusion.47
  947.9 9.8 fusion.843
  957.8 8.5 convert_bitcast_fusion.6
  966.3 10.0 convert_bitcast_fusion.5
  976.3 8.5 copy.901
  991.0 8.4 copy.902
  1029.7 6.3 copy.904
  1036.1 6.8 fusion.852
  1085.5 9.2 fusion.776
  1115.1 7.2 copy.876
  1122.3 7.2 copy.877
  1129.6 9.0 bitcast_reduce_fusion.2
  1138.6 8.0 copy.878
  1372.0 12.2 convert_reduce_fusion.6
  1384.1 9.2 convolution_convert_fusion.47
  1398.0 9.8 fusion.843
  1407.9 8.5 convert_bitcast_fusion.6
  1416.4 10.0 convert_bitcast_fusion.5
  1426.4 8.5 copy.901
  1434.9 6.4 reshape.1161
  1441.3 8.4 copy.902
  1479.8 6.3 copy.904
  1486.2 6.8 fusion.852
  1535.6 9.2 fusion.776
  1565.5 7.2 copy.876
  1572.7 7.2 copy.877
  1579.9 9.0 bitcast_reduce_fusion.2
  1588.9 8.0 copy.878
  1822.0 12.2 convert_reduce_fusion.6
  1834.3 9.2 convolution_convert_fusion.47
  1848.1 10.0 fusion.843
  1858.2 8.5 convert_bitcast_fusion.6
  1866.8 10.0 convert_bitcast_fusion.5
  1876.7 8.5 copy.901
  1891.4 8.4 copy.902
  1930.0 6.3 copy.904
  1936.3 6.8 fusion.852
  2009.4 41.7 %psum.23 = f32[]{:T(128)} all-reduce(f32[]{:T(128)} %get-tuple-element.2691), channel_id=1, replica_groups=mesh['crop'=8,'shard'=4] {'crop','shard'}, use_global_device_ids=true, to_apply=%region_94.95 | all-reduce | flops 1 | bytes 8 | tf_op jit(solution)/shard_map/psum | solution.py:302
  2051.2 125.9 %all-reduce.35.cloned.1.call-done = f32[14320,128]{1,0:T(8,128)} async-done(((f32[14320,128]{1,0:T(8,128)}), f32[14320,128]{1,0:T(8,128)}) %all-reduce.35.cloned.1.call-update) | async-done | bytes 7331856 | tf_op jit(solution)/shard_map/psum | solution.py:302
  2182.5 6.4 fusion.424
  (3239 shorter events, 1346.5 us)
Async XLA Ops:
  7.2 48.5 %all-gather.9.cloned.1.call-start = ((), (), s32[]{:S(2)}) async-start(), calls=%async_computation.3 | async-start | bytes 4587520 | tf_op jit(solution)/shard_map/all_gather | solution.py:259
  9.8 84.4 %all-gather.7.cloned.1.call-start = ((), (), s32[]{:S(2)}) async-start(), calls=%async_computation.1 | async-start | bytes 8192000 | tf_op jit(solution)/shard_map/all_gather | solution.py:261
  10.5 172.2 %all-gather.5.cloned.1.call-start = ((), (), s32[]{:S(2)}) async-start(), calls=%async_computation | async-start | bytes 16793600 | tf_op jit(solution)/shard_map/all_gather | solution.py:260
  11.3 2165.8 %all-reduce.35.cloned.1.call-start = ((), (), s32[]{:S(2)}) async-start(), calls=%async_computation.2 | async-start | bytes 14663680 | tf_op jit(solution)/shard_map/psum | solution.py:302
  75.7 107.1 %slice-start.7 = ((bf16[14320,128]{1,0:T(8,128)(2,1)}), bf16[65,128]{1,0:T(8,128)(2,1)S(1)}, s32[]{:S(2)}) async-start(bf16[14320,128]{1,0:T(8,128)(2,1)} %reshape.1091), calls=%async_computation.11 | async-start | bytes 36864 | tf_op jit(solution)/shard_map/slice | solution.py:62
  75.7 107.1 %copy-start.181 = (bf16[21,1280]{1,0:T(8,128)(2,1)S(1)}, bf16[21,1280]{1,0:T(8,128)(2,1)}, u32[]{:S(2)}) copy-start(bf16[21,1280]{1,0:T(8,128)(2,1)} %param.17) | copy-start | bytes 161284
  182.8 15.5 copy-start.109
  182.8 22.6 %copy-start.85 = (bf16[1280,256]{1,0:T(8,128)(2,1)}, bf16[1280,256]{1,0:T(8,128)(2,1)S(1)}, u32[]{:S(2)}) copy-start(bf16[1280,256]{1,0:T(8,128)(2,1)S(1)} %get-tuple-element.2565) | copy-start | bytes 1966084 | tf_op jit(solution)/shard_map/while
  182.8 23.2 %copy-start.91 = (bf16[256,256]{1,0:T(8,128)(2,1)}, bf16[256,256]{1,0:T(8,128)(2,1)S(1)}, u32[]{:S(2)}) copy-start(bf16[256,256]{1,0:T(8,128)(2,1)S(1)} %get-tuple-element.2569) | copy-start | bytes 393220 | tf_op jit(solution)/shard_map/while
  182.8 23.5 %copy-start.111 = (bf16[256,768]{1,0:T(8,128)(2,1)}, bf16[256,768]{1,0:T(8,128)(2,1)S(1)}, u32[]{:S(2)}) copy-start(bf16[256,768]{1,0:T(8,128)(2,1)S(1)} %get-tuple-element.2567) | copy-start | bytes 1179652 | tf_op jit(solution)/shard_map/while
  182.8 120.4 %copy-start.87 = (bf16[128,512]{1,0:T(8,128)(2,1)}, bf16[128,512]{1,0:T(8,128)(2,1)S(1)}, u32[]{:S(2)}) copy-start(bf16[128,512]{1,0:T(8,128)(2,1)S(1)} %get-tuple-element.2576) | copy-start | bytes 393220 | tf_op jit(solution)/shard_map/while
  185.5 27.0 %copy-start.229 = (f32[128]{0:T(128)}, f32[128]{0:T(128)S(1)}, u32[]{:S(2)}) copy-start(f32[128]{0:T(128)S(1)} %get-tuple-element.2268) | copy-start | bytes 1540 | tf_op jit(solution)/shard_map/while
  185.5 68.2 %copy-start.243 = (f32[128]{0:T(128)}, f32[128]{0:T(128)S(1)}, u32[]{:S(2)}) copy-start(f32[128]{0:T(128)S(1)} %get-tuple-element.2274) | copy-start | bytes 1540 | tf_op jit(solution)/shard_map/while
  185.5 75.0 %copy-start.227 = (f32[128]{0:T(128)}, f32[128]{0:T(128)S(1)}, u32[]{:S(2)}) copy-start(f32[128]{0:T(128)S(1)} %get-tuple-element.2279) | copy-start | bytes 1540 | tf_op jit(solution)/shard_map/while
  185.5 117.7 %copy-start.199 = (f32[128]{0:T(128)}, f32[128]{0:T(128)S(1)}, u32[]{:S(2)}) copy-start(f32[128]{0:T(128)S(1)} %get-tuple-element.2289) | copy-start | bytes 1540 | tf_op jit(solution)/shard_map/while
  187.4 18.7 copy-start.206
  187.4 19.0 copy-start.220
  188.5 65.2 %copy-start.13 = (f32[32,32,128]{2,1,0:T(8,128)}, f32[32,32,128]{2,1,0:T(8,128)S(1)}, u32[]{:S(2)}) copy-start(f32[32,32,128]{2,1,0:T(8,128)S(1)} %fusion.787) | copy-start | bytes 1572868 | tf_op jit(solution)/shard_map/while
  205.8 226.6 %copy-start.24 = (f32[4,32,256]{2,1,0:T(8,128)}, f32[4,32,256]{2,1,0:T(8,128)S(1)}, u32[]{:S(2)}) copy-start(f32[4,32,256]{2,1,0:T(8,128)S(1)} %get-tuple-element.2261) | copy-start | bytes 393220 | tf_op jit(solution)/shard_map/while
  210.1 43.6 %copy-start.6 = (f32[4,32,32,128]{3,2,1,0:T(8,128)}, f32[4,32,32,128]{3,2,1,0:T(8,128)S(1)}, u32[]{:S(2)}) copy-start(f32[4,32,32,128]{3,2,1,0:T(8,128)S(1)} %get-tuple-element.2267) | copy-start | bytes 6291460 | tf_op jit(solution)/shard_map/while
  629.2 15.5 copy-start.109
  629.2 22.6 %copy-start.85 = (bf16[1280,256]{1,0:T(8,128)(2,1)}, bf16[1280,256]{1,0:T(8,128)(2,1)S(1)}, u32[]{:S(2)}) copy-start(bf16[1280,256]{1,0:T(8,128)(2,1)S(1)} %get-tuple-element.2565) | copy-start | bytes 1966084 | tf_op jit(solution)/shard_map/while
  629.2 23.2 %copy-start.91 = (bf16[256,256]{1,0:T(8,128)(2,1)}, bf16[256,256]{1,0:T(8,128)(2,1)S(1)}, u32[]{:S(2)}) copy-start(bf16[256,256]{1,0:T(8,128)(2,1)S(1)} %get-tuple-element.2569) | copy-start | bytes 393220 | tf_op jit(solution)/shard_map/while
  629.2 23.5 %copy-start.111 = (bf16[256,768]{1,0:T(8,128)(2,1)}, bf16[256,768]{1,0:T(8,128)(2,1)S(1)}, u32[]{:S(2)}) copy-start(bf16[256,768]{1,0:T(8,128)(2,1)S(1)} %get-tuple-element.2567) | copy-start | bytes 1179652 | tf_op jit(solution)/shard_map/while
  629.2 120.1 %copy-start.87 = (bf16[128,512]{1,0:T(8,128)(2,1)}, bf16[128,512]{1,0:T(8,128)(2,1)S(1)}, u32[]{:S(2)}) copy-start(bf16[128,512]{1,0:T(8,128)(2,1)S(1)} %get-tuple-element.2576) | copy-start | bytes 393220 | tf_op jit(solution)/shard_map/while
  631.9 26.7 %copy-start.229 = (f32[128]{0:T(128)}, f32[128]{0:T(128)S(1)}, u32[]{:S(2)}) copy-start(f32[128]{0:T(128)S(1)} %get-tuple-element.2268) | copy-start | bytes 1540 | tf_op jit(solution)/shard_map/while
  631.9 67.9 %copy-start.243 = (f32[128]{0:T(128)}, f32[128]{0:T(128)S(1)}, u32[]{:S(2)}) copy-start(f32[128]{0:T(128)S(1)} %get-tuple-element.2274) | copy-start | bytes 1540 | tf_op jit(solution)/shard_map/while
  631.9 74.7 %copy-start.227 = (f32[128]{0:T(128)}, f32[128]{0:T(128)S(1)}, u32[]{:S(2)}) copy-start(f32[128]{0:T(128)S(1)} %get-tuple-element.2279) | copy-start | bytes 1540 | tf_op jit(solution)/shard_map/while
  631.9 117.4 %copy-start.199 = (f32[128]{0:T(128)}, f32[128]{0:T(128)S(1)}, u32[]{:S(2)}) copy-start(f32[128]{0:T(128)S(1)} %get-tuple-element.2289) | copy-start | bytes 1540 | tf_op jit(solution)/shard_map/while
  633.8 18.7 copy-start.206
  633.8 19.0 copy-start.220
  634.9 64.9 %copy-start.13 = (f32[32,32,128]{2,1,0:T(8,128)}, f32[32,32,128]{2,1,0:T(8,128)S(1)}, u32[]{:S(2)}) copy-start(f32[32,32,128]{2,1,0:T(8,128)S(1)} %fusion.787) | copy-start | bytes 1572868 | tf_op jit(solution)/shard_map/while
  652.2 227.2 %copy-start.24 = (f32[4,32,256]{2,1,0:T(8,128)}, f32[4,32,256]{2,1,0:T(8,128)S(1)}, u32[]{:S(2)}) copy-start(f32[4,32,256]{2,1,0:T(8,128)S(1)} %get-tuple-element.2261) | copy-start | bytes 393220 | tf_op jit(solution)/shard_map/while
  656.5 43.3 %copy-start.6 = (f32[4,32,32,128]{3,2,1,0:T(8,128)}, f32[4,32,32,128]{3,2,1,0:T(8,128)S(1)}, u32[]{:S(2)}) copy-start(f32[4,32,32,128]{3,2,1,0:T(8,128)S(1)} %get-tuple-element.2267) | copy-start | bytes 6291460 | tf_op jit(solution)/shard_map/while
  1079.2 15.5 copy-start.109
  1079.2 22.6 %copy-start.85 = (bf16[1280,256]{1,0:T(8,128)(2,1)}, bf16[1280,256]{1,0:T(8,128)(2,1)S(1)}, u32[]{:S(2)}) copy-start(bf16[1280,256]{1,0:T(8,128)(2,1)S(1)} %get-tuple-element.2565) | copy-start | bytes 1966084 | tf_op jit(solution)/shard_map/while
  1079.2 23.2 %copy-start.91 = (bf16[256,256]{1,0:T(8,128)(2,1)}, bf16[256,256]{1,0:T(8,128)(2,1)S(1)}, u32[]{:S(2)}) copy-start(bf16[256,256]{1,0:T(8,128)(2,1)S(1)} %get-tuple-element.2569) | copy-start | bytes 393220 | tf_op jit(solution)/shard_map/while
  1079.2 23.5 %copy-start.111 = (bf16[256,768]{1,0:T(8,128)(2,1)}, bf16[256,768]{1,0:T(8,128)(2,1)S(1)}, u32[]{:S(2)}) copy-start(bf16[256,768]{1,0:T(8,128)(2,1)S(1)} %get-tuple-element.2567) | copy-start | bytes 1179652 | tf_op jit(solution)/shard_map/while
  1079.2 120.5 %copy-start.87 = (bf16[128,512]{1,0:T(8,128)(2,1)}, bf16[128,512]{1,0:T(8,128)(2,1)S(1)}, u32[]{:S(2)}) copy-start(bf16[128,512]{1,0:T(8,128)(2,1)S(1)} %get-tuple-element.2576) | copy-start | bytes 393220 | tf_op jit(solution)/shard_map/while
  1081.9 26.8 %copy-start.229 = (f32[128]{0:T(128)}, f32[128]{0:T(128)S(1)}, u32[]{:S(2)}) copy-start(f32[128]{0:T(128)S(1)} %get-tuple-element.2268) | copy-start | bytes 1540 | tf_op jit(solution)/shard_map/while
  1081.9 67.9 %copy-start.243 = (f32[128]{0:T(128)}, f32[128]{0:T(128)S(1)}, u32[]{:S(2)}) copy-start(f32[128]{0:T(128)S(1)} %get-tuple-element.2274) | copy-start | bytes 1540 | tf_op jit(solution)/shard_map/while
  1081.9 74.8 %copy-start.227 = (f32[128]{0:T(128)}, f32[128]{0:T(128)S(1)}, u32[]{:S(2)}) copy-start(f32[128]{0:T(128)S(1)} %get-tuple-element.2279) | copy-start | bytes 1540 | tf_op jit(solution)/shard_map/while
  1081.9 117.8 %copy-start.199 = (f32[128]{0:T(128)}, f32[128]{0:T(128)S(1)}, u32[]{:S(2)}) copy-start(f32[128]{0:T(128)S(1)} %get-tuple-element.2289) | copy-start | bytes 1540 | tf_op jit(solution)/shard_map/while
  1083.8 18.7 copy-start.206
  1083.8 19.0 copy-start.220
  1084.9 65.0 %copy-start.13 = (f32[32,32,128]{2,1,0:T(8,128)}, f32[32,32,128]{2,1,0:T(8,128)S(1)}, u32[]{:S(2)}) copy-start(f32[32,32,128]{2,1,0:T(8,128)S(1)} %fusion.787) | copy-start | bytes 1572868 | tf_op jit(solution)/shard_map/while
  1102.2 227.4 %copy-start.24 = (f32[4,32,256]{2,1,0:T(8,128)}, f32[4,32,256]{2,1,0:T(8,128)S(1)}, u32[]{:S(2)}) copy-start(f32[4,32,256]{2,1,0:T(8,128)S(1)} %get-tuple-element.2261) | copy-start | bytes 393220 | tf_op jit(solution)/shard_map/while
  1106.5 43.4 %copy-start.6 = (f32[4,32,32,128]{3,2,1,0:T(8,128)}, f32[4,32,32,128]{3,2,1,0:T(8,128)S(1)}, u32[]{:S(2)}) copy-start(f32[4,32,32,128]{3,2,1,0:T(8,128)S(1)} %get-tuple-element.2267) | copy-start | bytes 6291460 | tf_op jit(solution)/shard_map/while
  1332.1 12.9 slice-start.5
  1529.3 15.5 copy-start.109
  1529.3 22.6 %copy-start.85 = (bf16[1280,256]{1,0:T(8,128)(2,1)}, bf16[1280,256]{1,0:T(8,128)(2,1)S(1)}, u32[]{:S(2)}) copy-start(bf16[1280,256]{1,0:T(8,128)(2,1)S(1)} %get-tuple-element.2565) | copy-start | bytes 1966084 | tf_op jit(solution)/shard_map/while
  1529.4 23.2 %copy-start.91 = (bf16[256,256]{1,0:T(8,128)(2,1)}, bf16[256,256]{1,0:T(8,128)(2,1)S(1)}, u32[]{:S(2)}) copy-start(bf16[256,256]{1,0:T(8,128)(2,1)S(1)} %get-tuple-element.2569) | copy-start | bytes 393220 | tf_op jit(solution)/shard_map/while
  1529.4 23.5 %copy-start.111 = (bf16[256,768]{1,0:T(8,128)(2,1)}, bf16[256,768]{1,0:T(8,128)(2,1)S(1)}, u32[]{:S(2)}) copy-start(bf16[256,768]{1,0:T(8,128)(2,1)S(1)} %get-tuple-element.2567) | copy-start | bytes 1179652 | tf_op jit(solution)/shard_map/while
  1529.4 120.4 %copy-start.87 = (bf16[128,512]{1,0:T(8,128)(2,1)}, bf16[128,512]{1,0:T(8,128)(2,1)S(1)}, u32[]{:S(2)}) copy-start(bf16[128,512]{1,0:T(8,128)(2,1)S(1)} %get-tuple-element.2576) | copy-start | bytes 393220 | tf_op jit(solution)/shard_map/while
  1532.1 27.0 %copy-start.229 = (f32[128]{0:T(128)}, f32[128]{0:T(128)S(1)}, u32[]{:S(2)}) copy-start(f32[128]{0:T(128)S(1)} %get-tuple-element.2268) | copy-start | bytes 1540 | tf_op jit(solution)/shard_map/while
  1532.1 68.2 %copy-start.243 = (f32[128]{0:T(128)}, f32[128]{0:T(128)S(1)}, u32[]{:S(2)}) copy-start(f32[128]{0:T(128)S(1)} %get-tuple-element.2274) | copy-start | bytes 1540 | tf_op jit(solution)/shard_map/while
  1532.1 75.0 %copy-start.227 = (f32[128]{0:T(128)}, f32[128]{0:T(128)S(1)}, u32[]{:S(2)}) copy-start(f32[128]{0:T(128)S(1)} %get-tuple-element.2279) | copy-start | bytes 1540 | tf_op jit(solution)/shard_map/while
  1532.1 117.7 %copy-start.199 = (f32[128]{0:T(128)}, f32[128]{0:T(128)S(1)}, u32[]{:S(2)}) copy-start(f32[128]{0:T(128)S(1)} %get-tuple-element.2289) | copy-start | bytes 1540 | tf_op jit(solution)/shard_map/while
  1534.0 18.7 copy-start.206
  1534.0 19.0 copy-start.220
  1535.0 65.2 %copy-start.13 = (f32[32,32,128]{2,1,0:T(8,128)}, f32[32,32,128]{2,1,0:T(8,128)S(1)}, u32[]{:S(2)}) copy-start(f32[32,32,128]{2,1,0:T(8,128)S(1)} %fusion.787) | copy-start | bytes 1572868 | tf_op jit(solution)/shard_map/while
  1552.4 227.5 %copy-start.24 = (f32[4,32,256]{2,1,0:T(8,128)}, f32[4,32,256]{2,1,0:T(8,128)S(1)}, u32[]{:S(2)}) copy-start(f32[4,32,256]{2,1,0:T(8,128)S(1)} %get-tuple-element.2261) | copy-start | bytes 393220 | tf_op jit(solution)/shard_map/while
  1556.7 43.6 %copy-start.6 = (f32[4,32,32,128]{3,2,1,0:T(8,128)}, f32[4,32,32,128]{3,2,1,0:T(8,128)S(1)}, u32[]{:S(2)}) copy-start(f32[4,32,32,128]{3,2,1,0:T(8,128)S(1)} %get-tuple-element.2267) | copy-start | bytes 6291460 | tf_op jit(solution)/shard_map/while
  2051.2 131.4 %copy-start.127 = (f32[3580,128]{1,0:T(8,128)S(1)}, f32[3580,128]{1,0:T(8,128)}, u32[]{:S(2)}) copy-start(f32[3580,128]{1,0:T(8,128)} %param.13) | copy-start | bytes 5498884
  (1010 other events, 3419.0 us)
Sparse Core Ops, SparseCore 0:
  10.1 34.4 all-gather.8
  46.2 47.9 all-gather.6
  95.8 86.9 all-gather.4
  2008.8 168.2 all-reduce.34
where the time goes:
time: 2210 us; the launch traced here: 2200 us
  matrix products  784 us (35%)
  local copies, waits for them, and re-layouts  618 us (28%)
  other arithmetic  437 us (20%)
  waiting for transfers between devices  229 us (10%)
  blocking collectives  84.3 us (4%)
  loops' own time  25.5 us (1%)
    dot_general x344, matrix products, product(): jnp.einsum(form, left.astype(jnp.bfloat16), right.astype(jnp.bfloat16), p...  780 us
    psum x1, waiting for transfers between devices, local(): summed, loss = lax.psum((grad_rows, loss_part), ('crop', 'shard'))  126 us
    convert_element_type x56, local copies, waits for them, and re-layouts, product(): right.astype(jnp.bfloat16)  125 us
    convert_element_type x28, local copies, waits for them, and re-layouts, product(): left.astype(jnp.bfloat16)  89.2 us
    all_gather x1, waiting for transfers between devices, local(): lax.all_gather(plm_first, 'shard', axis=0, tiled=True)  88.5 us
    dot_general x28, local copies, waits for them, and re-layouts, product(): jnp.einsum(form, left.astype(jnp.bfloat16), right.astype(jnp.bfloat16), p...  84.9 us
    reduce_sum x28, other arithmetic, layer_norm(): return centred * lax.rsqrt(spread + 1e-05) * gain  80.5 us
    while x2096, local copies, waits for them, and re-layouts  50 us
  transfers between devices with their start and end apart: 4, of which 3 were waited for; matrix products, arithmetic and copies ran while one was open for 1% of the time, Pallas kernels for 0%

commit v1 on v0

--- a/solution.py
+++ b/solution.py
@@ -255,9 +255,23 @@
     resolved,
     coords,
 ):
+
+    def turn_rates(piece_in, which_dim):
+        latest = jax.lax.axis_size("shard")
+        z_new, carry_in = (latest, jax.lax.axis_index("shard"))
+        arr_next, x_next = (piece_in, 1)
+        while x_next < z_new:
+            built = tuple(((p, p ^ x_next) for p in range(z_new)))
+            kept_arr = jax.lax.ppermute(arr_next, "shard", built)
+            w2 = jnp.concatenate([arr_next, kept_arr], axis=which_dim)
+            current_block = jnp.concatenate([kept_arr, arr_next], axis=which_dim)
+            arr_next = jnp.where(carry_in & x_next == 0, w2, current_block)
+            x_next = 2 * x_next
+        return arr_next
+
     gathered, frozen_first, frozen_second = (
         lax.all_gather(master.astype(jnp.bfloat16), "shard", axis=0, tiled=True),
-        lax.all_gather(plm_first, "shard", axis=0, tiled=True),
+        turn_rates(plm_first, which_dim=0),
         lax.all_gather(plm_second, "shard", axis=0, tiled=True),
     )
     params = unpack(gathered.astype(jnp.float32).reshape(-1))

time: 2210 us -> 2330 us (1.054)
  blocking collectives: 84.3 us -> 269 us
  waiting for transfers between devices: 229 us -> 131 us
  other arithmetic: 437 us -> 465 us
    psum x1, blocking collectives: 42.6 us -> 228 us  [local(): total_pairs = lax.psum(local_pairs, ('crop', 'shard'))]
    all_gather x1 -> x0, waiting for transfers between devices: 88.5 us -> none  [local(): lax.all_gather(plm_first, 'shard', axis=0, tiled=True)]
    select_n x0 -> x2, other arithmetic: none -> 24.7 us  [turn_rates(): arr_next = jnp.where(carry_in & x_next == 0, w2, current_block)]
    while x2096 -> x2088, local copies, waits for them, and re-layouts: 50 us -> 49.4 us
  transfers between devices with their start and end apart: 4 -> 5, of which waited for: 3 -> 2; matrix products, arithmetic and copies ran while one was open for 1% -> 2% of each run, Pallas kernels for 0% -> 0%
where the time goes in v1:
time: 2330 us; the launch traced here: 2320 us
  matrix products  786 us (34%)
  local copies, waits for them, and re-layouts  617 us (26%)
  other arithmetic  465 us (20%)
  blocking collectives  269 us (12%)
  waiting for transfers between devices  131 us (6%)
  loops' own time  26 us (1%)
    dot_general x344, matrix products, product(): jnp.einsum(form, left.astype(jnp.bfloat16), right.astype(jnp.bfloat16), p...  782 us
    psum x1, blocking collectives, local(): total_pairs = lax.psum(local_pairs, ('crop', 'shard'))  228 us
    psum x1, waiting for transfers between devices, local(): summed, loss = lax.psum((grad_rows, loss_part), ('crop', 'shard'))  125 us
    convert_element_type x56, local copies, waits for them, and re-layouts, product(): right.astype(jnp.bfloat16)  125 us
    convert_element_type x28, local copies, waits for them, and re-layouts, product(): left.astype(jnp.bfloat16)  88.9 us
    dot_general x28, local copies, waits for them, and re-layouts, product(): jnp.einsum(form, left.astype(jnp.bfloat16), right.astype(jnp.bfloat16), p...  84.8 us
    reduce_sum x28, other arithmetic, layer_norm(): return centred * lax.rsqrt(spread + 1e-05) * gain  80.4 us
    while x2088, local copies, waits for them, and re-layouts  49.4 us
  transfers between devices with their start and end apart: 5, of which 2 were waited for; matrix products, arithmetic and copies ran while one was open for 2% of the time, Pallas kernels for 0%

profile of v1, /device:TPU:0, one launch (start us, length us, event | category | flops | bytes accessed | tf_op | source)
XLA Modules:
  0.0 2315.6 jit_solution(12886252837886479977)
XLA Ops:
  16.2 7.9 maximum_select_fusion.1
  28.6 227.5 %psum.21 = f32[]{:T(128)} all-reduce(f32[]{:T(128)} %multiply_reduce_fusion.27), channel_id=1, replica_groups=mesh['crop'=8,'shard'=4] {'crop','shard'}, use_global_device_ids=true, to_apply=%region_2.3 | all-reduce | flops 1 | bytes 8 | tf_op jit(solution)/shard_map/psum | solution.py:280
  281.5 16.7 maximum_select_fusion
  298.2 1806.8 %while.60 = (s32[]{:T(128)}, f32[6,256]{1,0:T(8,128)}, f32[6,128]{1,0:T(8,128)}, f32[256,3]{0,1:T(4,128)}, f32[128,8]{0,1:T(8,128)}, /*index=5*/f32[1280,256]{1,...) while((s32[]{:T(128)}, f32[6,256]{1,0:T(8,128)}, ...), condition=%wide.region_91.92_spmd.clone, body=%wide.region_3.91_spmd.clone.sunk | while | flops 12452269056 | bytes 911617344 | solution.py:313
  305.5 9.2 fusion.776
  335.4 7.2 copy.876
  342.6 7.2 copy.877
  349.8 9.0 bitcast_reduce_fusion.2
  358.7 8.0 copy.878
  589.4 12.2 convert_reduce_fusion.6
  601.7 9.2 convolution_convert_fusion.47
  615.5 10.0 fusion.843
  625.6 8.5 convert_bitcast_fusion.6
  634.1 10.0 convert_bitcast_fusion.5
  644.1 8.5 copy.901
  658.8 8.4 copy.902
  696.2 6.4 copy.904
  702.6 6.8 fusion.852
  752.9 9.2 fusion.776
  782.5 7.2 copy.876
  789.7 7.2 copy.877
  796.9 9.0 bitcast_reduce_fusion.2
  805.9 8.0 copy.878
  1039.4 12.4 convert_reduce_fusion.6
  1051.8 9.2 convolution_convert_fusion.47
  1065.7 9.8 fusion.843
  1075.5 8.5 convert_bitcast_fusion.6
  1084.1 10.0 convert_bitcast_fusion.5
  1094.0 8.5 copy.901
  1108.8 8.4 copy.902
  1147.5 6.4 copy.904
  1153.8 6.8 fusion.852
  1203.9 9.2 fusion.776
  1233.5 7.2 copy.876
  1240.7 7.2 copy.877
  1247.9 9.0 bitcast_reduce_fusion.2
  1256.9 8.0 copy.878
  1490.6 12.2 convert_reduce_fusion.6
  1502.8 9.2 convolution_convert_fusion.47
  1516.7 9.8 fusion.843
  1526.6 8.5 convert_bitcast_fusion.6
  1535.1 10.0 convert_bitcast_fusion.5
  1545.1 8.5 copy.901
  1553.6 6.4 reshape.1161
  1560.0 8.4 copy.902
  1598.5 6.4 copy.904
  1604.9 6.8 fusion.852
  1655.0 9.2 fusion.776
  1684.8 7.2 copy.876
  1692.0 7.2 copy.877
  1699.2 9.0 bitcast_reduce_fusion.2
  1708.2 8.0 copy.878
  1941.7 12.2 convert_reduce_fusion.6
  1953.9 9.2 convolution_convert_fusion.47
  1967.7 10.0 fusion.843
  1977.9 8.5 convert_bitcast_fusion.6
  1986.4 10.0 convert_bitcast_fusion.5
  1996.3 8.5 copy.901
  2011.0 8.4 copy.902
  2049.6 6.4 copy.904
  2055.9 6.8 fusion.852
  2129.0 41.8 %psum.23 = f32[]{:T(128)} all-reduce(f32[]{:T(128)} %get-tuple-element.2630), channel_id=1, replica_groups=mesh['crop'=8,'shard'=4] {'crop','shard'}, use_global_device_ids=true, to_apply=%region_94.95 | all-reduce | flops 1 | bytes 8 | tf_op jit(solution)/shard_map/psum | solution.py:316
  2170.8 125.1 %all-reduce.35.cloned.1.call-done = f32[14320,128]{1,0:T(8,128)} async-done(((f32[14320,128]{1,0:T(8,128)}), f32[14320,128]{1,0:T(8,128)}) %all-reduce.35.cloned.1.call-update) | async-done | bytes 7331856 | tf_op jit(solution)/shard_map/psum | solution.py:316
  2301.4 6.4 fusion.424
  (3234 shorter events, 1358.1 us)
Async XLA Ops:
  7.2 249.9 %all-gather.6.cloned.1.call-start = ((), (), s32[]{:S(2)}) async-start(), calls=%async_computation.2 | async-start | bytes 4587520 | tf_op jit(solution)/shard_map/all_gather | solution.py:273
  9.9 288.3 %all-gather.4.cloned.1.call-start = ((), (), s32[]{:S(2)}) async-start(), calls=%async_computation | async-start | bytes 8192000 | tf_op jit(solution)/shard_map/all_gather | solution.py:275
  10.0 6.3 collective-permute-start
  10.7 2285.3 %all-reduce.35.cloned.1.call-start = ((), (), s32[]{:S(2)}) async-start(), calls=%async_computation.1 | async-start | bytes 14663680 | tf_op jit(solution)/shard_map/psum | solution.py:316
  10.7 16.4 copy-start.270
  24.2 257.3 %collective-permute-start.1 = (bf16[640,5248]{1,0:T(8,128)(2,1)}, bf16[640,5248]{1,0:T(8,128)(2,1)}, u32[]{:S(2)}, u32[]{:S(2)}) collective-permute-start(bf16[640,5248]{1,0:T(8,128)(2,1)} %maximum_select_fusion.1), channel_id=1, source_target_pairs={{0,2},{1,3},{2,0},{3,1},{4,6},{5,7},{6,4},{7,5},{8,10},{9,11},{10,... | collective-permute-start | bytes 20152328 | tf_op jit(solution)/shard_map/ppermute | solution.py:265
  281.4 16.7 slice-start.7
  281.4 16.8 copy-start.182
  298.5 23.2 %copy-start.85 = (bf16[1280,256]{1,0:T(8,128)(2,1)}, bf16[1280,256]{1,0:T(8,128)(2,1)S(1)}, u32[]{:S(2)}) copy-start(bf16[1280,256]{1,0:T(8,128)(2,1)S(1)} %get-tuple-element.2565) | copy-start | bytes 1966084 | tf_op jit(solution)/shard_map/while
  298.6 23.9 %copy-start.91 = (bf16[256,256]{1,0:T(8,128)(2,1)}, bf16[256,256]{1,0:T(8,128)(2,1)S(1)}, u32[]{:S(2)}) copy-start(bf16[256,256]{1,0:T(8,128)(2,1)S(1)} %get-tuple-element.2569) | copy-start | bytes 393220 | tf_op jit(solution)/shard_map/while
  298.6 24.1 %copy-start.111 = (bf16[256,768]{1,0:T(8,128)(2,1)}, bf16[256,768]{1,0:T(8,128)(2,1)S(1)}, u32[]{:S(2)}) copy-start(bf16[256,768]{1,0:T(8,128)(2,1)S(1)} %get-tuple-element.2567) | copy-start | bytes 1179652 | tf_op jit(solution)/shard_map/while
  298.6 121.0 %copy-start.87 = (bf16[128,512]{1,0:T(8,128)(2,1)}, bf16[128,512]{1,0:T(8,128)(2,1)S(1)}, u32[]{:S(2)}) copy-start(bf16[128,512]{1,0:T(8,128)(2,1)S(1)} %get-tuple-element.2576) | copy-start | bytes 393220 | tf_op jit(solution)/shard_map/while
  301.9 27.1 %copy-start.230 = (f32[128]{0:T(128)}, f32[128]{0:T(128)S(1)}, u32[]{:S(2)}) copy-start(f32[128]{0:T(128)S(1)} %get-tuple-element.2268) | copy-start | bytes 1540 | tf_op jit(solution)/shard_map/while
  301.9 68.2 %copy-start.244 = (f32[128]{0:T(128)}, f32[128]{0:T(128)S(1)}, u32[]{:S(2)}) copy-start(f32[128]{0:T(128)S(1)} %get-tuple-element.2274) | copy-start | bytes 1540 | tf_op jit(solution)/shard_map/while
  301.9 75.1 %copy-start.228 = (f32[128]{0:T(128)}, f32[128]{0:T(128)S(1)}, u32[]{:S(2)}) copy-start(f32[128]{0:T(128)S(1)} %get-tuple-element.2279) | copy-start | bytes 1540 | tf_op jit(solution)/shard_map/while
  301.9 117.8 %copy-start.200 = (f32[128]{0:T(128)}, f32[128]{0:T(128)S(1)}, u32[]{:S(2)}) copy-start(f32[128]{0:T(128)S(1)} %get-tuple-element.2289) | copy-start | bytes 1540 | tf_op jit(solution)/shard_map/while
  303.8 18.7 copy-start.207
  303.8 19.0 copy-start.221
  304.9 65.2 %copy-start.13 = (f32[32,32,128]{2,1,0:T(8,128)}, f32[32,32,128]{2,1,0:T(8,128)S(1)}, u32[]{:S(2)}) copy-start(f32[32,32,128]{2,1,0:T(8,128)S(1)} %fusion.787) | copy-start | bytes 1572868 | tf_op jit(solution)/shard_map/while
  322.2 227.1 %copy-start.24 = (f32[4,32,256]{2,1,0:T(8,128)}, f32[4,32,256]{2,1,0:T(8,128)S(1)}, u32[]{:S(2)}) copy-start(f32[4,32,256]{2,1,0:T(8,128)S(1)} %get-tuple-element.2261) | copy-start | bytes 393220 | tf_op jit(solution)/shard_map/while
  326.5 43.6 %copy-start.6 = (f32[4,32,32,128]{3,2,1,0:T(8,128)}, f32[4,32,32,128]{3,2,1,0:T(8,128)S(1)}, u32[]{:S(2)}) copy-start(f32[4,32,32,128]{3,2,1,0:T(8,128)S(1)} %get-tuple-element.2267) | copy-start | bytes 6291460 | tf_op jit(solution)/shard_map/while
  746.0 16.1 copy-start.109
  746.0 23.2 %copy-start.85 = (bf16[1280,256]{1,0:T(8,128)(2,1)}, bf16[1280,256]{1,0:T(8,128)(2,1)S(1)}, u32[]{:S(2)}) copy-start(bf16[1280,256]{1,0:T(8,128)(2,1)S(1)} %get-tuple-element.2565) | copy-start | bytes 1966084 | tf_op jit(solution)/shard_map/while
  746.0 23.9 %copy-start.91 = (bf16[256,256]{1,0:T(8,128)(2,1)}, bf16[256,256]{1,0:T(8,128)(2,1)S(1)}, u32[]{:S(2)}) copy-start(bf16[256,256]{1,0:T(8,128)(2,1)S(1)} %get-tuple-element.2569) | copy-start | bytes 393220 | tf_op jit(solution)/shard_map/while
  746.0 24.2 %copy-start.111 = (bf16[256,768]{1,0:T(8,128)(2,1)}, bf16[256,768]{1,0:T(8,128)(2,1)S(1)}, u32[]{:S(2)}) copy-start(bf16[256,768]{1,0:T(8,128)(2,1)S(1)} %get-tuple-element.2567) | copy-start | bytes 1179652 | tf_op jit(solution)/shard_map/while
  746.1 120.7 %copy-start.87 = (bf16[128,512]{1,0:T(8,128)(2,1)}, bf16[128,512]{1,0:T(8,128)(2,1)S(1)}, u32[]{:S(2)}) copy-start(bf16[128,512]{1,0:T(8,128)(2,1)S(1)} %get-tuple-element.2576) | copy-start | bytes 393220 | tf_op jit(solution)/shard_map/while
  749.3 26.7 %copy-start.230 = (f32[128]{0:T(128)}, f32[128]{0:T(128)S(1)}, u32[]{:S(2)}) copy-start(f32[128]{0:T(128)S(1)} %get-tuple-element.2268) | copy-start | bytes 1540 | tf_op jit(solution)/shard_map/while
  749.3 67.9 %copy-start.244 = (f32[128]{0:T(128)}, f32[128]{0:T(128)S(1)}, u32[]{:S(2)}) copy-start(f32[128]{0:T(128)S(1)} %get-tuple-element.2274) | copy-start | bytes 1540 | tf_op jit(solution)/shard_map/while
  749.3 74.8 %copy-start.228 = (f32[128]{0:T(128)}, f32[128]{0:T(128)S(1)}, u32[]{:S(2)}) copy-start(f32[128]{0:T(128)S(1)} %get-tuple-element.2279) | copy-start | bytes 1540 | tf_op jit(solution)/shard_map/while
  749.3 117.5 %copy-start.200 = (f32[128]{0:T(128)}, f32[128]{0:T(128)S(1)}, u32[]{:S(2)}) copy-start(f32[128]{0:T(128)S(1)} %get-tuple-element.2289) | copy-start | bytes 1540 | tf_op jit(solution)/shard_map/while
  751.3 18.7 copy-start.207
  751.3 19.0 copy-start.221
  752.3 64.9 %copy-start.13 = (f32[32,32,128]{2,1,0:T(8,128)}, f32[32,32,128]{2,1,0:T(8,128)S(1)}, u32[]{:S(2)}) copy-start(f32[32,32,128]{2,1,0:T(8,128)S(1)} %fusion.787) | copy-start | bytes 1572868 | tf_op jit(solution)/shard_map/while
  769.7 227.5 %copy-start.24 = (f32[4,32,256]{2,1,0:T(8,128)}, f32[4,32,256]{2,1,0:T(8,128)S(1)}, u32[]{:S(2)}) copy-start(f32[4,32,256]{2,1,0:T(8,128)S(1)} %get-tuple-element.2261) | copy-start | bytes 393220 | tf_op jit(solution)/shard_map/while
  773.9 43.3 %copy-start.6 = (f32[4,32,32,128]{3,2,1,0:T(8,128)}, f32[4,32,32,128]{3,2,1,0:T(8,128)S(1)}, u32[]{:S(2)}) copy-start(f32[4,32,32,128]{3,2,1,0:T(8,128)S(1)} %get-tuple-element.2267) | copy-start | bytes 6291460 | tf_op jit(solution)/shard_map/while
  1196.9 16.1 copy-start.109
  1196.9 23.2 %copy-start.85 = (bf16[1280,256]{1,0:T(8,128)(2,1)}, bf16[1280,256]{1,0:T(8,128)(2,1)S(1)}, u32[]{:S(2)}) copy-start(bf16[1280,256]{1,0:T(8,128)(2,1)S(1)} %get-tuple-element.2565) | copy-start | bytes 1966084 | tf_op jit(solution)/shard_map/while
  1196.9 23.9 %copy-start.91 = (bf16[256,256]{1,0:T(8,128)(2,1)}, bf16[256,256]{1,0:T(8,128)(2,1)S(1)}, u32[]{:S(2)}) copy-start(bf16[256,256]{1,0:T(8,128)(2,1)S(1)} %get-tuple-element.2569) | copy-start | bytes 393220 | tf_op jit(solution)/shard_map/while
  1197.0 24.2 %copy-start.111 = (bf16[256,768]{1,0:T(8,128)(2,1)}, bf16[256,768]{1,0:T(8,128)(2,1)S(1)}, u32[]{:S(2)}) copy-start(bf16[256,768]{1,0:T(8,128)(2,1)S(1)} %get-tuple-element.2567) | copy-start | bytes 1179652 | tf_op jit(solution)/shard_map/while
  1197.0 121.1 %copy-start.87 = (bf16[128,512]{1,0:T(8,128)(2,1)}, bf16[128,512]{1,0:T(8,128)(2,1)S(1)}, u32[]{:S(2)}) copy-start(bf16[128,512]{1,0:T(8,128)(2,1)S(1)} %get-tuple-element.2576) | copy-start | bytes 393220 | tf_op jit(solution)/shard_map/while
  1200.2 26.8 %copy-start.230 = (f32[128]{0:T(128)}, f32[128]{0:T(128)S(1)}, u32[]{:S(2)}) copy-start(f32[128]{0:T(128)S(1)} %get-tuple-element.2268) | copy-start | bytes 1540 | tf_op jit(solution)/shard_map/while
  1200.2 67.9 %copy-start.244 = (f32[128]{0:T(128)}, f32[128]{0:T(128)S(1)}, u32[]{:S(2)}) copy-start(f32[128]{0:T(128)S(1)} %get-tuple-element.2274) | copy-start | bytes 1540 | tf_op jit(solution)/shard_map/while
  1200.2 74.9 %copy-start.228 = (f32[128]{0:T(128)}, f32[128]{0:T(128)S(1)}, u32[]{:S(2)}) copy-start(f32[128]{0:T(128)S(1)} %get-tuple-element.2279) | copy-start | bytes 1540 | tf_op jit(solution)/shard_map/while
  1200.2 117.8 %copy-start.200 = (f32[128]{0:T(128)}, f32[128]{0:T(128)S(1)}, u32[]{:S(2)}) copy-start(f32[128]{0:T(128)S(1)} %get-tuple-element.2289) | copy-start | bytes 1540 | tf_op jit(solution)/shard_map/while
  1202.2 18.7 copy-start.207
  1202.2 19.0 copy-start.221
  1203.3 64.9 %copy-start.13 = (f32[32,32,128]{2,1,0:T(8,128)}, f32[32,32,128]{2,1,0:T(8,128)S(1)}, u32[]{:S(2)}) copy-start(f32[32,32,128]{2,1,0:T(8,128)S(1)} %fusion.787) | copy-start | bytes 1572868 | tf_op jit(solution)/shard_map/while
  1220.6 227.7 %copy-start.24 = (f32[4,32,256]{2,1,0:T(8,128)}, f32[4,32,256]{2,1,0:T(8,128)S(1)}, u32[]{:S(2)}) copy-start(f32[4,32,256]{2,1,0:T(8,128)S(1)} %get-tuple-element.2261) | copy-start | bytes 393220 | tf_op jit(solution)/shard_map/while
  1224.8 43.4 %copy-start.6 = (f32[4,32,32,128]{3,2,1,0:T(8,128)}, f32[4,32,32,128]{3,2,1,0:T(8,128)S(1)}, u32[]{:S(2)}) copy-start(f32[4,32,32,128]{3,2,1,0:T(8,128)S(1)} %get-tuple-element.2267) | copy-start | bytes 6291460 | tf_op jit(solution)/shard_map/while
  1648.0 16.1 copy-start.109
  1648.0 23.2 %copy-start.85 = (bf16[1280,256]{1,0:T(8,128)(2,1)}, bf16[1280,256]{1,0:T(8,128)(2,1)S(1)}, u32[]{:S(2)}) copy-start(bf16[1280,256]{1,0:T(8,128)(2,1)S(1)} %get-tuple-element.2565) | copy-start | bytes 1966084 | tf_op jit(solution)/shard_map/while
  1648.1 23.9 %copy-start.91 = (bf16[256,256]{1,0:T(8,128)(2,1)}, bf16[256,256]{1,0:T(8,128)(2,1)S(1)}, u32[]{:S(2)}) copy-start(bf16[256,256]{1,0:T(8,128)(2,1)S(1)} %get-tuple-element.2569) | copy-start | bytes 393220 | tf_op jit(solution)/shard_map/while
  1648.1 24.2 %copy-start.111 = (bf16[256,768]{1,0:T(8,128)(2,1)}, bf16[256,768]{1,0:T(8,128)(2,1)S(1)}, u32[]{:S(2)}) copy-start(bf16[256,768]{1,0:T(8,128)(2,1)S(1)} %get-tuple-element.2567) | copy-start | bytes 1179652 | tf_op jit(solution)/shard_map/while
  1648.1 121.0 %copy-start.87 = (bf16[128,512]{1,0:T(8,128)(2,1)}, bf16[128,512]{1,0:T(8,128)(2,1)S(1)}, u32[]{:S(2)}) copy-start(bf16[128,512]{1,0:T(8,128)(2,1)S(1)} %get-tuple-element.2576) | copy-start | bytes 393220 | tf_op jit(solution)/shard_map/while
  1651.3 27.0 %copy-start.230 = (f32[128]{0:T(128)}, f32[128]{0:T(128)S(1)}, u32[]{:S(2)}) copy-start(f32[128]{0:T(128)S(1)} %get-tuple-element.2268) | copy-start | bytes 1540 | tf_op jit(solution)/shard_map/while
  1651.3 68.2 %copy-start.244 = (f32[128]{0:T(128)}, f32[128]{0:T(128)S(1)}, u32[]{:S(2)}) copy-start(f32[128]{0:T(128)S(1)} %get-tuple-element.2274) | copy-start | bytes 1540 | tf_op jit(solution)/shard_map/while
  1651.3 75.1 %copy-start.228 = (f32[128]{0:T(128)}, f32[128]{0:T(128)S(1)}, u32[]{:S(2)}) copy-start(f32[128]{0:T(128)S(1)} %get-tuple-element.2279) | copy-start | bytes 1540 | tf_op jit(solution)/shard_map/while
  1651.3 117.7 %copy-start.200 = (f32[128]{0:T(128)}, f32[128]{0:T(128)S(1)}, u32[]{:S(2)}) copy-start(f32[128]{0:T(128)S(1)} %get-tuple-element.2289) | copy-start | bytes 1540 | tf_op jit(solution)/shard_map/while
  1653.3 18.7 copy-start.207
  1653.3 19.0 copy-start.221
  1654.4 65.2 %copy-start.13 = (f32[32,32,128]{2,1,0:T(8,128)}, f32[32,32,128]{2,1,0:T(8,128)S(1)}, u32[]{:S(2)}) copy-start(f32[32,32,128]{2,1,0:T(8,128)S(1)} %fusion.787) | copy-start | bytes 1572868 | tf_op jit(solution)/shard_map/while
  1671.7 227.8 %copy-start.24 = (f32[4,32,256]{2,1,0:T(8,128)}, f32[4,32,256]{2,1,0:T(8,128)S(1)}, u32[]{:S(2)}) copy-start(f32[4,32,256]{2,1,0:T(8,128)S(1)} %get-tuple-element.2261) | copy-start | bytes 393220 | tf_op jit(solution)/shard_map/while
  1676.0 43.6 %copy-start.6 = (f32[4,32,32,128]{3,2,1,0:T(8,128)}, f32[4,32,32,128]{3,2,1,0:T(8,128)S(1)}, u32[]{:S(2)}) copy-start(f32[4,32,32,128]{3,2,1,0:T(8,128)S(1)} %get-tuple-element.2267) | copy-start | bytes 6291460 | tf_op jit(solution)/shard_map/while
  2170.8 130.5 %copy-start.127 = (f32[3580,128]{1,0:T(8,128)S(1)}, f32[3580,128]{1,0:T(8,128)}, u32[]{:S(2)}) copy-start(f32[3580,128]{1,0:T(8,128)} %param.13) | copy-start | bytes 5498884
  (1007 other events, 3453.0 us)
Sparse Core Ops, SparseCore 0:
  10.1 48.7 all-gather.5
  60.5 82.3 all-gather.3
  2128.4 167.4 all-reduce.34
